TPU v7x, 512 devices: a whole 4x8x8 slice. The times are simulated.
512 devices in a mesh: row: 32 (over z, y_hi), col: 16 (over y_lo, x, core).
Axes of the slice: x: 4, y: 8 (y_hi: 4, y_lo: 2; y = y_hi * 2 + y_lo), z: 8, core: 2. Of those that a mesh axis runs over, the one named last changes fastest.
Arguments:
- inverse_block: bfloat16 [20480, 20480], P('row', 'col')
- factor_cols: bfloat16 [3, 20480, 512], P(None, 'col', 'row'), may hold values from -6 to 6
- occupancy: int32 [3, 160], replicated, may hold values 0 or 1
- row_block: int32 [3, 160], replicated, may hold values from 0 to 159, each once within a row
- coupling: bfloat16 [2, 512, 512], replicated, may hold values from -0.25 to 0.25
- diag_inverse: float32 [3, 512, 512], P(None, None, 'col'), may hold values from -6 to 6
Outputs:
- columns: float32 [3, 20480, 512], P(None, ('row', 'col'))
- diagonals: float32 [3, 512, 512], P(None, None, 'col')
Inputs may be any that keep to these rules, and one draw needn't show every extreme that they name: `row_block`: each row names every one of the 160 row blocks exactly once.
All inputs are finite; a program needn't handle non-finite values.
Results may differ from a plain program's by a relative error of at most 0.0003.
Values may be sent and summed in bfloat16 or wider, within the bound.
A program may use at most 64 MiB of HBM per device.

v0:
```python
import jax
import jax.numpy as jnp
from jax import lax
from jax.sharding import PartitionSpec as P

highest = lax.Precision.HIGHEST


def routed(gathered, occupancy, row_block, nblocks):
    count = gathered.shape[0]
    width_part = gathered.shape[1] // (nblocks * 128)
    blocks = gathered.reshape(count, nblocks, 128, width_part)
    levels = lax.broadcasted_iota(jnp.int32, (count, nblocks, nblocks), 1)
    picks = ((row_block[:, None, :] == levels) & (occupancy[:, None, :] > 0)).astype(jnp.bfloat16)
    placed = jnp.einsum("kqb,kbtx->kxqt", picks, blocks, preferred_element_type=jnp.float32)
    return placed.astype(jnp.bfloat16).reshape(count, width_part, nblocks * 128)


def split_rows(placed, column, row_parts, col_parts, tile):
    count, width_part, total = placed.shape
    span = total // col_parts
    column_part = lax.dynamic_slice_in_dim(placed, column * span, span, 2)
    grid = placed.reshape(count, width_part, row_parts, col_parts, tile)
    mine = lax.dynamic_index_in_dim(grid, column, 3, keepdims=False)
    return (column_part, jnp.transpose(mine, (0, 2, 1, 3)))


def make_term(inverse_block, column_full):
    return lax.dot_general(
        inverse_block, column_full, (((1,), (2,)), ((), ())), preferred_element_type=jnp.float32
    )


def local_step(summed, own_rows, previous, link, diag_part, column, row_first, rows_total):
    if link is None:
        coupled = jnp.zeros_like(summed)
    else:
        coupled = jnp.dot(previous, link.astype(jnp.float32), precision=highest)
    current = -(summed + coupled)
    own = own_rows.astype(jnp.float32)
    inner = jnp.dot(own, current, precision=highest) - jnp.dot(coupled.T, own.T, precision=highest)
    width = summed.shape[1]
    diag_cols = diag_part.shape[1]
    embedded = lax.dynamic_update_slice(
        jnp.zeros((width, width), jnp.float32), diag_part, (0, column * diag_cols)
    )
    return (current, row_first * embedded - inner / rows_total)


def chain_diag(total, chain_prev, link):
    if link is None:
        return total
    link_wide = link.astype(jnp.float32)
    return total + jnp.dot(
        link_wide.T, jnp.dot(chain_prev, link_wide, precision=highest), precision=highest
    )


def per_device(inverse_block, factor_cols, occupancy, row_block, coupling, diag_inverse):
    column = lax.axis_index("col")
    row_first = (lax.axis_index("row") == 0).astype(jnp.float32)
    row_parts = lax.axis_size("row")
    col_parts = lax.axis_size("col")
    local_rows = inverse_block.shape[0]
    rows_total = local_rows * row_parts
    supers, span, width_part = factor_cols.shape
    width = width_part * row_parts
    tile = local_rows // col_parts
    nblocks = occupancy.shape[1]
    diag_cols = diag_inverse.shape[2]
    flat = factor_cols.reshape(supers, span * width_part)
    column_list = []
    partial_list = []
    previous = None
    for position in range(supers):
        gathered = lax.all_gather(flat[position : position + 1], "col", axis=1, tiled=True)
        placed = routed(
            gathered,
            occupancy[position : position + 1],
            row_block[position : position + 1],
            nblocks,
        )
        column_part, outgoing = split_rows(placed, column, row_parts, col_parts, tile)
        column_full = lax.all_gather(column_part, "row", axis=1, tiled=True)
        arrived = lax.all_to_all(outgoing, "row", split_axis=1, concat_axis=1, tiled=True)
        summed = lax.psum_scatter(
            make_term(inverse_block, column_full), "col", scatter_dimension=0, tiled=True
        )
        link = None if position == 0 else coupling[position - 1]
        current, partial_value = local_step(
            summed[:, 0, :],
            arrived.reshape(width, tile),
            previous,
            link,
            diag_inverse[position],
            column,
            row_first,
            rows_total,
        )
        column_list.append(current)
        partial_list.append(partial_value)
        previous = current
    diag_list = []
    totals = lax.psum(jnp.stack(partial_list), ("row", "col"))
    chain_prev = None
    for position in range(supers):
        link = None if position == 0 else coupling[position - 1]
        diag_now = chain_diag(totals[position], chain_prev, link)
        diag_list.append(lax.dynamic_slice_in_dim(diag_now, column * diag_cols, diag_cols, 1))
        chain_prev = diag_now
    diagonals = jnp.stack(diag_list)
    return (jnp.stack(column_list), diagonals)


def solution(mesh):
    in_specs = (P("row", "col"), P(None, "col", "row"), P(), P(), P(), P(None, None, "col"))
    out_specs = (P(None, ("row", "col"), None), P(None, None, "col"))
    return jax.shard_map(
        per_device, mesh=mesh, in_specs=in_specs, out_specs=out_specs, check_vma=False
    )
```

profile of v0, /device:TPU:17, one launch (start us, length us, event | category | flops | bytes accessed | tf_op | source)
XLA Modules:
  0.0 766.2 jit_solution(6525715898854247528)
XLA Ops:
  8.6 24.0 %all_gather.20 = bf16[1,327680]{1,0:T(2,128)(2,1)S(1)} all-gather(bf16[1,20480]{1,0:T(2,128)(2,1)S(1)} %slice.69), channel_id=1, replica_groups=mesh['row'=32,'col'=16] {'col'}, dimensions={1}, use_global_device_ids=true | all-gather | bytes 696320 | tf_op jit(solution)/shard_map/all_gather | solution.py:76
  32.6 14.5 %reduce.3 = bf16[327680]{0:T(1024)(128)(2,1)} reduce(bf16[1,327680]{1,0:T(2,128)(2,1)S(1)} %all_gather.20, bf16[]{:T(256)} %constant.52), dimensions={0}, to_apply=%all_gather.20.reduce_sub_computation | reduce | bytes 1310722 | tf_op jit(solution)/shard_map/all_gather | solution.py:76
  47.1 6.4 reshape.188
  53.6 4.0 copy.64
  59.4 22.1 %all_gather.22 = bf16[1,327680]{1,0:T(2,128)(2,1)} all-gather(bf16[1,20480]{1,0:T(2,128)(2,1)S(1)} %slice.74), channel_id=1, replica_groups=mesh['row'=32,'col'=16] {'col'}, dimensions={1}, use_global_device_ids=true | all-gather | bytes 696320 | tf_op jit(solution)/shard_map/all_gather | solution.py:76
  81.5 14.6 %reduce.5 = bf16[327680]{0:T(1024)(128)(2,1)S(1)} reduce(bf16[1,327680]{1,0:T(2,128)(2,1)} %all_gather.22, bf16[]{:T(256)} %constant.52), dimensions={0}, to_apply=%all_gather.22.reduce_sub_computation | reduce | bytes 1310722 | tf_op jit(solution)/shard_map/all_gather | solution.py:76
  96.2 4.9 reshape.191
  101.1 4.9 copy.67
  110.4 29.4 %all_gather.18 = bf16[1,327680]{1,0:T(2,128)(2,1)} all-gather(bf16[1,20480]{1,0:T(2,128)(2,1)S(1)} %slice.65), channel_id=1, replica_groups=mesh['row'=32,'col'=16] {'col'}, dimensions={1}, use_global_device_ids=true | all-gather | bytes 696320 | tf_op jit(solution)/shard_map/all_gather | solution.py:76
  139.9 15.5 %reduce.1 = bf16[327680]{0:T(1024)(128)(2,1)} reduce(bf16[1,327680]{1,0:T(2,128)(2,1)} %all_gather.18, bf16[]{:T(256)} %constant.52), dimensions={0}, to_apply=%all_gather.18.reduce_sub_computation | reduce | bytes 1310722 | tf_op jit(solution)/shard_map/all_gather | solution.py:76
  155.3 6.5 reshape.185
  161.9 4.9 copy.61
  180.2 42.0 %all-gather.8.cloned.1.call-done = bf16[1,512,1280]{2,1,0:T(8,128)(2,1)} async-done(((bf16[1,16,1280]{2,1,0:T(8,128)(2,1)}), bf16[1,512,1280]{2,1,0:T(8,128)(2,1)}) %all-gather.8.cloned.1.call-update) | async-done | bytes 1310736 | tf_op jit(solution)/shard_map/all_gather | solution.py:84
  229.5 76.1 %all-gather.4.cloned.1.call-done = bf16[1,512,1280]{2,1,0:T(8,128)(2,1)} async-done(((bf16[1,16,1280]{2,1,0:T(8,128)(2,1)}), bf16[1,512,1280]{2,1,0:T(8,128)(2,1)}) %all-gather.4.cloned.1.call-update) | async-done | bytes 1310736 | tf_op jit(solution)/shard_map/all_gather | solution.py:84
  313.2 4.1 reshape_reshape.10
  317.3 4.1 reshape_reshape.11
  324.7 6.9 all-to-all-start.1
  331.6 4.1 reshape_reshape.9
  336.7 4.3 all-to-all-done.1
  340.9 7.4 all-to-all-start.2
  350.8 6.8 all-to-all-done.2
  357.7 5.5 all-to-all-start
  375.5 78.5 %all-reduce.9.cloned.1.call-done = (f32[640,1,512]{2,1,0:T(1,128)}, f32[640,1,512]{2,1,0:T(1,128)}, f32[640,1,512]{2,1,0:T(1,128)}) async-done(((f32[640,1,512]{2,1,0:T(1,128)}, f32[640,1,512]{2,1,0:T(1,128)}, f32[640,1,512]{2,1,0:T(1,128)}), (f32[640,1,512]{2,1,0:T(1,128)}, f32[640,1,512]{2,1,0:T(1,128)}, f32[640,1,512]{2,1,0:T(1,128)})) %all-reduce.9.cloned.1.call-update) | async-done | bytes 3932176
  465.7 284.7 %all-reduce.7.cloned.1.call-done = f32[3,512,512]{2,1,0:T(8,128)} async-done(((f32[3,512,512]{2,1,0:T(8,128)}), f32[3,512,512]{2,1,0:T(8,128)}) %all-reduce.7.cloned.1.call-update) | async-done | bytes 3145744 | tf_op jit(solution)/shard_map/psum | solution.py:104
  (114 shorter events, 74.7 us)
Async XLA Ops:
  7.2 165.6 %copy-start = (bf16[640,1280]{1,0:T(8,128)(2,1)S(1)}, bf16[640,1280]{1,0:T(8,128)(2,1)}, u32[]{:S(2)}) copy-start(bf16[640,1280]{1,0:T(8,128)(2,1)} %param.6) | copy-start | bytes 4915204
  7.2 165.5 %all-gather.6.cloned.1.call-start = ((), (), s32[]{:S(2)}) async-start(), calls=%async_computation.4 | async-start | bytes 1351680 | tf_op jit(solution)/shard_map/all_gather | solution.py:84
  53.5 4.0 copy-start.12
  53.5 4.0 copy-start.13
  58.9 163.2 %all-gather.8.cloned.1.call-start = ((), (), s32[]{:S(2)}) async-start(), calls=%async_computation.5 | async-start | bytes 1351680 | tf_op jit(solution)/shard_map/all_gather | solution.py:84
  109.9 195.7 %all-gather.4.cloned.1.call-start = ((), (), s32[]{:S(2)}) async-start(), calls=%async_computation.3 | async-start | bytes 1351680 | tf_op jit(solution)/shard_map/all_gather | solution.py:84
  172.6 281.4 %all-reduce.9.cloned.1.call-start = ((), (), s32[]{:S(2)}) async-start(), calls=%async_computation.7 | async-start | bytes 7864320
  321.4 10.1 %copy-start.3 = (bf16[1,16,160,128]{3,2,1,0:T(8,128)(2,1)S(1)}, bf16[1,16,160,128]{3,2,1,0:T(8,128)(2,1)}, u32[]{:S(2)}) copy-start(bf16[1,16,160,128]{3,2,1,0:T(8,128)(2,1)} %fusion.13) | copy-start | bytes 1966084
  324.7 16.3 %all-to-all-start.1 = ((bf16[32,2,320]{2,1,0:T(2,128)(2,1)}), bf16[32,2,320]{2,1,0:T(2,128)(2,1)S(1)}, u32[]{:S(2)}, u32[]{:S(2)}) async-start(bf16[32,2,320]{2,1,0:T(2,128)(2,1)} %reshape.211), calls=%async_computation.1 | async-start | bytes 98304 | tf_op jit(solution)/shard_map/all_to_all | solution.py:85
  335.7 27.5 %copy-start.11 = (f32[3,512,32]{1,2,0:T(8,128)S(1)}, f32[3,512,32]{1,2,0:T(8,128)}, u32[]{:S(2)}) copy-start(f32[3,512,32]{1,2,0:T(8,128)} %param.11) | copy-start | bytes 589828
  340.9 16.7 %all-to-all-start.2 = ((bf16[32,2,320]{2,1,0:T(2,128)(2,1)}), bf16[32,2,320]{2,1,0:T(2,128)(2,1)S(1)}, u32[]{:S(2)}, u32[]{:S(2)}) async-start(bf16[32,2,320]{2,1,0:T(2,128)(2,1)} %reshape.209), calls=%async_computation.2 | async-start | bytes 98304 | tf_op jit(solution)/shard_map/all_to_all | solution.py:85
  357.7 16.6 %all-to-all-start = ((bf16[32,2,320]{2,1,0:T(2,128)(2,1)}), bf16[32,2,320]{2,1,0:T(2,128)(2,1)S(1)}, u32[]{:S(2)}, u32[]{:S(2)}) async-start(bf16[32,2,320]{2,1,0:T(2,128)(2,1)} %reshape.213), calls=%async_computation | async-start | bytes 98304 | tf_op jit(solution)/shard_map/all_to_all | solution.py:85
  363.1 387.2 %all-reduce.7.cloned.1.call-start = ((), (), s32[]{:S(2)}) async-start(), calls=%async_computation.6 | async-start | bytes 6291456 | tf_op jit(solution)/shard_map/psum | solution.py:104
  368.0 3.5 copy-start.7
  370.5 1.1 copy-start.9
  371.6 84.2 %copy-start.2 = (bf16[2,512,512]{2,1,0:T(8,128)(2,1)S(1)}, bf16[2,512,512]{2,1,0:T(8,128)(2,1)}, u32[]{:S(2)}) copy-start(bf16[2,512,512]{2,1,0:T(8,128)(2,1)} %param.10) | copy-start | bytes 3145732
  374.0 1.0 copy-start.5
  456.2 1.8 copy-start.8
  458.8 1.2 copy-start.10
  460.0 1.2 copy-start.6
  755.9 1.9 copy-start.4
  758.0 1.4 copy-start.1
Sparse Core Ops, SparseCore 0:
  59.0 80.0 all-gather.5
  142.2 79.8 all-gather.7
  225.9 79.7 all-gather.3
  313.3 140.6 all-reduce.8
  464.1 286.2 all-reduce.6
where the time goes:
time: 774 us; the launch traced here: 766 us
  waiting for transfers between devices  492 us (64%)
  local copies, waits for them, and re-layouts  86.9 us (11%)
  blocking collectives  75.5 us (10%)
  other arithmetic  50.2 us (6%)
  matrix products  25.9 us (3%)
  starting transfers between devices  19.9 us (3%)
  between operations  15.2 us (2%)
    psum x1, waiting for transfers between devices, per_device(): totals = lax.psum(jnp.stack(partial_list), ('row', 'col'))  285 us
    all_gather x3, waiting for transfers between devices, per_device(): column_full = lax.all_gather(column_part, 'row', axis=1, tiled=True)  118 us
    unnamed x6, waiting for transfers between devices  78.6 us
    all_gather x3, blocking collectives, per_device(): lax.all_gather(flat[position:position + 1], 'col', axis=1, tiled=True)  75.5 us
    all_gather x3, other arithmetic, per_device(): lax.all_gather(flat[position:position + 1], 'col', axis=1, tiled=True)  44.6 us
    another operation x9, local copies, waits for them, and re-layouts  32 us
    all_to_all x3, starting transfers between devices, per_device(): lax.all_to_all(outgoing, 'row', split_axis=1, concat_axis=1, tiled=True)  19.7 us
  transfers between devices with their start and end apart: 8, of which 6 were waited for; matrix products, arithmetic and copies ran while one was open for 14% of the time, Pallas kernels for 0%

commit v1 on v0

--- a/solution.py
+++ b/solution.py
@@ -82,7 +82,12 @@
         )
         column_part, outgoing = split_rows(placed, column, row_parts, col_parts, tile)
         column_full = lax.all_gather(column_part, "row", axis=1, tiled=True)
-        arrived = lax.all_to_all(outgoing, "row", split_axis=1, concat_axis=1, tiled=True)
+        arrived = jnp.concatenate(
+            lax.all_to_all(
+                jnp.stack(jnp.split(outgoing, lax.axis_size("row"), axis=1), axis=0), "row", 0, 0
+            ),
+            axis=1,
+        )
         summed = lax.psum_scatter(
             make_term(inverse_block, column_full), "col", scatter_dimension=0, tiled=True
         )

time: 774 us -> 777 us (level)
  starting transfers between devices: 19.9 us -> 27.7 us
    unnamed x6, waiting for transfers between devices: 78.6 us -> 105 us
    all_gather x3, waiting for transfers between devices: 118 us -> 96.2 us  [per_device(): column_full = lax.all_gather(column_part, 'row', axis=1, tiled=True)]
    another operation x9 -> x13, local copies, waits for them, and re-layouts: 32 us -> 30.7 us
  transfers between devices with their start and end apart: 8 -> 8, of which waited for: 6 -> 5; matrix products, arithmetic and copies ran while one was open for 14% -> 13% of each run, Pallas kernels for 0% -> 0%
where the time goes in v1:
time: 777 us; the launch traced here: 770 us
  waiting for transfers between devices  495 us (64%)
  local copies, waits for them, and re-layouts  86.8 us (11%)
  blocking collectives  72.7 us (9%)
  other arithmetic  48 us (6%)
  starting transfers between devices  27.7 us (4%)
  matrix products  23.9 us (3%)
  between operations  15.5 us (2%)
    psum x1, waiting for transfers between devices, per_device(): totals = lax.psum(jnp.stack(partial_list), ('row', 'col'))  286 us
    unnamed x6, waiting for transfers between devices  105 us
    all_gather x3, waiting for transfers between devices, per_device(): column_full = lax.all_gather(column_part, 'row', axis=1, tiled=True)  96.2 us
    all_gather x3, blocking collectives, per_device(): lax.all_gather(flat[position:position + 1], 'col', axis=1, tiled=True)  72.7 us
    all_gather x3, other arithmetic, per_device(): lax.all_gather(flat[position:position + 1], 'col', axis=1, tiled=True)  43.7 us
    another operation x9, local copies, waits for them, and re-layouts  30.6 us
    all_to_all x3, starting transfers between devices, per_device(): lax.all_to_all(jnp.stack(jnp.split(outgoing, lax.axis_size('row'), axis=1...  27.1 us
  transfers between devices with their start and end apart: 8, of which 5 were waited for; matrix products, arithmetic and copies ran while one was open for 13% of the time, Pallas kernels for 0%

profile of v1, /device:TPU:17, one launch (start us, length us, event | category | flops | bytes accessed | tf_op | source)
XLA Modules:
  0.0 769.8 jit_solution(13061373277158321488)
XLA Ops:
  8.6 24.0 %all_gather.18 = bf16[1,327680]{1,0:T(2,128)(2,1)S(1)} all-gather(bf16[1,20480]{1,0:T(2,128)(2,1)S(1)} %slice.65), channel_id=1, replica_groups=mesh['row'=32,'col'=16] {'col'}, dimensions={1}, use_global_device_ids=true | all-gather | bytes 696320 | tf_op jit(solution)/shard_map/all_gather | solution.py:76
  32.6 14.5 %reduce.1 = bf16[327680]{0:T(1024)(128)(2,1)} reduce(bf16[1,327680]{1,0:T(2,128)(2,1)S(1)} %all_gather.18, bf16[]{:T(256)} %constant.52), dimensions={0}, to_apply=%all_gather.18.reduce_sub_computation | reduce | bytes 1310722 | tf_op jit(solution)/shard_map/all_gather | solution.py:76
  47.1 6.5 reshape.176
  53.5 4.0 copy.2005
  59.4 21.9 %all_gather.20 = bf16[1,327680]{1,0:T(2,128)(2,1)} all-gather(bf16[1,20480]{1,0:T(2,128)(2,1)S(1)} %slice.69), channel_id=1, replica_groups=mesh['row'=32,'col'=16] {'col'}, dimensions={1}, use_global_device_ids=true | all-gather | bytes 696320 | tf_op jit(solution)/shard_map/all_gather | solution.py:76
  81.3 14.6 %reduce.3 = bf16[327680]{0:T(1024)(128)(2,1)S(1)} reduce(bf16[1,327680]{1,0:T(2,128)(2,1)} %all_gather.20, bf16[]{:T(256)} %constant.52), dimensions={0}, to_apply=%all_gather.20.reduce_sub_computation | reduce | bytes 1310722 | tf_op jit(solution)/shard_map/all_gather | solution.py:76
  95.9 5.0 reshape.179
  101.0 4.9 copy.2010
  109.8 4.1 reshape_reshape.20
  114.4 26.8 %all_gather.22 = bf16[1,327680]{1,0:T(2,128)(2,1)} all-gather(bf16[1,20480]{1,0:T(2,128)(2,1)S(1)} %slice.74), channel_id=1, replica_groups=mesh['row'=32,'col'=16] {'col'}, dimensions={1}, use_global_device_ids=true | all-gather | bytes 696320 | tf_op jit(solution)/shard_map/all_gather | solution.py:76
  141.1 14.6 %reduce.5 = bf16[327680]{0:T(1024)(128)(2,1)S(1)} reduce(bf16[1,327680]{1,0:T(2,128)(2,1)} %all_gather.22, bf16[]{:T(256)} %constant.52), dimensions={0}, to_apply=%all_gather.22.reduce_sub_computation | reduce | bytes 1310722 | tf_op jit(solution)/shard_map/all_gather | solution.py:76
  155.8 5.0 reshape.182
  160.8 4.9 copy.2017
  167.1 4.1 reshape_reshape.22
  174.8 14.7 %all-to-all-start.2 = ((bf16[32,2,320]{2,1,0:T(2,128)(2,1)}), bf16[32,2,320]{2,1,0:T(2,128)(2,1)S(1)}, u32[]{:S(2)}, u32[]{:S(2)}) async-start(bf16[32,2,320]{2,1,0:T(2,128)(2,1)} %reshape.197), calls=%async_computation.2 | async-start | bytes 98304 | tf_op jit(solution)/shard_map/all_to_all | solution.py:86
  192.6 4.1 reshape_reshape.18
  203.8 17.9 %all-gather.6.cloned.1.call-done = bf16[1,512,1280]{2,1,0:T(8,128)(2,1)} async-done(((bf16[1,16,1280]{2,1,0:T(8,128)(2,1)}), bf16[1,512,1280]{2,1,0:T(8,128)(2,1)}) %all-gather.6.cloned.1.call-update) | async-done | bytes 1310736 | tf_op jit(solution)/shard_map/all_gather | solution.py:84
  226.3 78.3 %all-gather.8.cloned.1.call-done = bf16[1,512,1280]{2,1,0:T(8,128)(2,1)} async-done(((bf16[1,16,1280]{2,1,0:T(8,128)(2,1)}), bf16[1,512,1280]{2,1,0:T(8,128)(2,1)}) %all-gather.8.cloned.1.call-update) | async-done | bytes 1310736 | tf_op jit(solution)/shard_map/all_gather | solution.py:84
  310.4 6.9 all-to-all-start.1
  318.1 8.5 %all-to-all-done.1 = bf16[32,2,320]{2,1,0:T(2,128)(2,1)S(1)} async-done(((bf16[32,2,320]{2,1,0:T(2,128)(2,1)}), bf16[32,2,320]{2,1,0:T(2,128)(2,1)S(1)}, u32[]{:S(2)}, u32[]{:S(2)}) %all-to-all-start.1) | async-done | bytes 40992 | tf_op jit(solution)/shard_map/all_to_all | solution.py:86
  326.6 5.5 all-to-all-start
  344.6 104.8 %all-reduce.9.cloned.1.call-done = (f32[640,1,512]{2,1,0:T(1,128)}, f32[640,1,512]{2,1,0:T(1,128)}, f32[640,1,512]{2,1,0:T(1,128)}) async-done(((f32[640,1,512]{2,1,0:T(1,128)}, f32[640,1,512]{2,1,0:T(1,128)}, f32[640,1,512]{2,1,0:T(1,128)}), (f32[640,1,512]{2,1,0:T(1,128)}, f32[640,1,512]{2,1,0:T(1,128)}, f32[640,1,512]{2,1,0:T(1,128)})) %all-reduce.9.cloned.1.call-update) | async-done | bytes 3932176
  459.9 285.6 %all-reduce.7.cloned.1.call-done = f32[3,512,512]{2,1,0:T(8,128)} async-done(((f32[3,512,512]{2,1,0:T(8,128)}), f32[3,512,512]{2,1,0:T(8,128)}) %all-reduce.7.cloned.1.call-update) | async-done | bytes 3145744 | tf_op jit(solution)/shard_map/psum | solution.py:109
  745.5 3.5 fusion.65
  (214 shorter events, 69.7 us)
Async XLA Ops:
  7.2 191.9 %copy-start = (bf16[640,1280]{1,0:T(8,128)(2,1)S(1)}, bf16[640,1280]{1,0:T(8,128)(2,1)}, u32[]{:S(2)}) copy-start(bf16[640,1280]{1,0:T(8,128)(2,1)} %param.6) | copy-start | bytes 4915204
  7.2 191.9 %all-gather.4.cloned.1.call-start = ((), (), s32[]{:S(2)}) async-start(), calls=%async_computation.3 | async-start | bytes 1351680 | tf_op jit(solution)/shard_map/all_gather | solution.py:84
  53.5 4.0 copy-start.11
  53.5 4.0 copy-start.12
  58.9 162.8 %all-gather.6.cloned.1.call-start = ((), (), s32[]{:S(2)}) async-start(), calls=%async_computation.4 | async-start | bytes 1351680 | tf_op jit(solution)/shard_map/all_gather | solution.py:84
  174.8 135.6 %all-to-all-start.2 = ((bf16[32,2,320]{2,1,0:T(2,128)(2,1)}), bf16[32,2,320]{2,1,0:T(2,128)(2,1)S(1)}, u32[]{:S(2)}, u32[]{:S(2)}) async-start(bf16[32,2,320]{2,1,0:T(2,128)(2,1)} %reshape.197), calls=%async_computation.2 | async-start | bytes 98304 | tf_op jit(solution)/shard_map/all_to_all | solution.py:86
  189.5 115.2 %all-gather.8.cloned.1.call-start = ((), (), s32[]{:S(2)}) async-start(), calls=%async_computation.5 | async-start | bytes 1351680 | tf_op jit(solution)/shard_map/all_gather | solution.py:84
  192.1 257.3 %all-reduce.9.cloned.1.call-start = ((), (), s32[]{:S(2)}) async-start(), calls=%async_computation.7 | async-start | bytes 7864320
  309.4 23.0 %copy-start.10 = (f32[3,512,32]{1,2,0:T(8,128)S(1)}, f32[3,512,32]{1,2,0:T(8,128)}, u32[]{:S(2)}) copy-start(f32[3,512,32]{1,2,0:T(8,128)} %param.11) | copy-start | bytes 589828
  310.4 16.2 %all-to-all-start.1 = ((bf16[32,2,320]{2,1,0:T(2,128)(2,1)}), bf16[32,2,320]{2,1,0:T(2,128)(2,1)S(1)}, u32[]{:S(2)}, u32[]{:S(2)}) async-start(bf16[32,2,320]{2,1,0:T(2,128)(2,1)} %reshape.199), calls=%async_computation.1 | async-start | bytes 98304 | tf_op jit(solution)/shard_map/all_to_all | solution.py:86
  326.6 16.8 %all-to-all-start = ((bf16[32,2,320]{2,1,0:T(2,128)(2,1)}), bf16[32,2,320]{2,1,0:T(2,128)(2,1)S(1)}, u32[]{:S(2)}, u32[]{:S(2)}) async-start(bf16[32,2,320]{2,1,0:T(2,128)(2,1)} %reshape.201), calls=%async_computation | async-start | bytes 98304 | tf_op jit(solution)/shard_map/all_to_all | solution.py:86
  332.1 413.4 %all-reduce.7.cloned.1.call-start = ((), (), s32[]{:S(2)}) async-start(), calls=%async_computation.6 | async-start | bytes 6291456 | tf_op jit(solution)/shard_map/psum | solution.py:109
  337.2 2.4 copy-start.6
  339.6 1.0 copy-start.8
  340.7 111.4 %copy-start.2 = (bf16[2,512,512]{2,1,0:T(8,128)(2,1)S(1)}, bf16[2,512,512]{2,1,0:T(8,128)(2,1)}, u32[]{:S(2)}) copy-start(bf16[2,512,512]{2,1,0:T(8,128)(2,1)} %param.10) | copy-start | bytes 3145732
  343.1 1.0 copy-start.4
  452.8 1.2 copy-start.7
  454.1 1.2 copy-start.9
  455.3 1.2 copy-start.5
  750.4 2.3 copy-start.3
  757.0 6.1 copy-start.1
Sparse Core Ops, SparseCore 0:
  59.0 80.0 all-gather.3
  142.3 79.3 all-gather.5
  224.9 79.7 all-gather.7
  309.5 139.8 all-reduce.8
  459.3 286.1 all-reduce.6
